TPU v7x, 32 devices: a whole 2x2x4 slice. The times are simulated.
32 devices in a mesh: child: 2 (over y), row: 4 (over x, core), col: 4 (over z).
Axes of the slice: x: 2, y: 2, z: 4, core: 2. Of those that a mesh axis runs over, the one named last changes fastest.
Arguments:
- child_blocks: float32 [2, 4096, 4096], P('child', 'row', 'col'), as said below
- child_panels: bfloat16 [2, 4096, 1024], P('child', 'row'), may hold values from -0.1875 to 0.1875
- child_patterns: int32 [2, 16, 16], replicated, may hold values from 0 to 1, as said below
- child_maps: int32 [2, 16], replicated, may hold values from 0 to 23, as said below
- parent_place: int32 [24], replicated, may hold values from 0 to 23, as said below
- parent_front: float32 [6144, 6144], P(('child', 'row'), 'col'), as said below
Outputs:
- factored: float32 [6144, 6144], P(('child', 'row'), 'col')
Inputs may be any that keep to these rules, and one draw needn't show every extreme that they name: `parent_place`: a permutation. The entries of one child are distinct; within each aligned block of 4 entries of one child, the values parent_place[child_maps[c, i]] // 6 are distinct. `child_patterns`: symmetric in its two tile dimensions, with ones on the diagonal. `child_blocks`: each child's block is symmetric. `parent_front`: symmetric; the diagonal entries inside stored tiles (parent_place[0], parent_place[0]) and (parent_place[1], parent_place[1]) lie between 200 and 400.
All inputs are finite; a program needn't handle non-finite values.
Results may differ from a plain program's by a relative error of at most 0.0003.
Values may be sent and summed in bfloat16 or wider, within the bound.
A program may use at most 128 MiB of HBM per device.

v0:
```python
import jax
import jax.numpy as jnp
from jax import lax
from jax.sharding import PartitionSpec as P

TILE = 256
PANEL = 512


def spread(block, axis, source):
    block = jnp.where(lax.axis_index(axis) == source, block, jnp.zeros_like(block))
    return lax.psum(block, axis)


def lookup(lookup_table, positions):
    matches = positions[:, None] == jnp.arange(lookup_table.shape[0], dtype=jnp.int32)[None, :]
    return jnp.sum(jnp.where(matches, lookup_table[None, :], 0), axis=1)


def find_owner(slot_list, targets):
    matches = targets[:, None] == slot_list[None, :]
    located = jnp.any(matches, axis=1)
    chosen = jnp.sum(
        jnp.where(matches, jnp.arange(slot_list.shape[0], dtype=jnp.int32)[None, :], 0), axis=1
    )
    return (located, chosen)


def select_tiles(source, located, chosen, axis_pos):
    selected = jnp.take(source, chosen, axis=axis_pos)
    dims_shape = [1] * source.ndim
    dims_shape[axis_pos] = located.shape[0]
    return jnp.where(located.reshape(dims_shape), selected, jnp.zeros((), source.dtype))


def body(child_blocks, child_panels, child_patterns, child_maps, parent_place, parent_front):
    child_index = lax.axis_index("child")
    row_index = lax.axis_index("row")
    col_index = lax.axis_index("col")
    row_count = lax.axis_size("row")
    col_count = lax.axis_size("col")
    group_count = lax.axis_size(("child", "row"))
    own_block = child_blocks[0]
    block_width = own_block.shape[0]
    tiles_dev = block_width // TILE
    rows_dev = parent_front.shape[0] // TILE
    cols_dev = parent_front.shape[1] // TILE
    own_panel = child_panels[0]
    partner = spread(own_panel, "row", col_index)
    product = lax.dot_general(
        own_panel, partner, (((1,), (1,)), ((), ())), preferred_element_type=jnp.float32
    )
    pattern = lax.dynamic_index_in_dim(child_patterns, child_index, 0, keepdims=False)
    pattern = lax.dynamic_slice(
        pattern, (row_index * tiles_dev, col_index * tiles_dev), (tiles_dev, tiles_dev)
    ).astype(jnp.float32)
    update = (own_block - product).reshape(tiles_dev, TILE, tiles_dev, TILE) * pattern[
        :, None, :, None
    ]
    slot_table = jnp.stack(
        [lookup(parent_place, child_maps[0]), lookup(parent_place, child_maps[1])]
    )
    own_slots = lax.dynamic_index_in_dim(slot_table, child_index, 0, keepdims=False)
    row_slots = lax.dynamic_slice_in_dim(own_slots, row_index * tiles_dev, tiles_dev)
    col_slots = lax.dynamic_slice_in_dim(own_slots, col_index * tiles_dev, tiles_dev)
    group_index = child_index * row_count + row_index
    row_targets = group_index * rows_dev + jnp.arange(rows_dev, dtype=jnp.int32)
    col_targets = col_index * cols_dev + jnp.arange(cols_dev, dtype=jnp.int32)
    group_ids = jnp.arange(group_count, dtype=jnp.int32)
    column_ids = jnp.arange(col_count, dtype=jnp.int32)
    located, chosen = find_owner(col_slots // cols_dev, column_ids)
    outgoing = select_tiles(update.reshape(block_width, tiles_dev, TILE), located, chosen, 1)
    incoming = lax.all_to_all(outgoing, "col", split_axis=1, concat_axis=1, tiled=True)
    located, chosen = find_owner(own_slots, col_targets)
    placed = select_tiles(incoming, located, chosen // tiles_dev, 1).reshape(
        tiles_dev, TILE, cols_dev * TILE
    )
    located, chosen = find_owner(row_slots // rows_dev, group_ids)
    outgoing_rows = select_tiles(placed, located, chosen, 0)
    incoming_rows = lax.all_to_all(
        outgoing_rows, ("child", "row"), split_axis=0, concat_axis=0, tiled=True
    )
    contribution = jnp.zeros((rows_dev, TILE, cols_dev * TILE), jnp.float32)
    for member in range(2):
        located, chosen = find_owner(slot_table[member], row_targets)
        sender = member * row_count + chosen // tiles_dev
        contribution = contribution + select_tiles(incoming_rows, located, sender, 0)
    assembled = parent_front + contribution.reshape(parent_front.shape)
    panel_slots = parent_place[0:2]
    col_local = panel_slots // cols_dev == col_index
    col_pos = panel_slots % cols_dev
    row_local = panel_slots // rows_dev == group_index
    row_pos = panel_slots % rows_dev
    front_tiles = assembled.reshape(rows_dev * TILE, cols_dev, TILE)
    column = select_tiles(front_tiles, col_local, col_pos, 1).reshape(rows_dev * TILE, PANEL)
    diagonal_part = select_tiles(
        column.reshape(rows_dev, TILE, PANEL), row_local, row_pos, 0
    ).reshape(PANEL, PANEL)
    panel_column = lax.psum(column, "col")
    diagonal_block = lax.psum(diagonal_part, ("child", "row", "col"))
    factor = jnp.linalg.cholesky(diagonal_block)
    panel_rows = lax.linalg.triangular_solve(
        factor, panel_column, left_side=False, lower=True, transpose_a=True
    )
    halves = []
    for member in range(2):
        halves.append(spread(panel_rows, ("child", "row"), 2 * col_index + member))
    panel_cols = jnp.concatenate(halves, axis=0)
    result = assembled - lax.dot_general(
        panel_rows,
        panel_cols,
        (((1,), (1,)), ((), ())),
        precision=lax.Precision.HIGHEST,
        preferred_element_type=jnp.float32,
    )
    result_tiles = result.reshape(rows_dev * TILE, cols_dev, TILE)
    tile_positions = jnp.arange(cols_dev, dtype=jnp.int32)
    for member in range(2):
        chosen_cols = jnp.logical_and(tile_positions == col_pos[member], col_local[member])
        result_tiles = jnp.where(
            chosen_cols[None, :, None],
            panel_rows[:, None, member * TILE : (member + 1) * TILE],
            result_tiles,
        )
    return result_tiles.reshape(parent_front.shape)


def solution(mesh):
    return jax.shard_map(
        body,
        mesh=mesh,
        in_specs=(
            P("child", "row", "col"),
            P("child", "row", None),
            P(),
            P(),
            P(),
            P(("child", "row"), "col"),
        ),
        out_specs=P(("child", "row"), "col"),
        check_vma=False,
    )
```

profile of v0, /device:TPU:0, one launch (start us, length us, event | category | flops | bytes accessed | tf_op | source)
XLA Modules:
  0.0 784.7 jit_solution(8666867808019406183)
XLA Ops:
  6.5 3.0 bitcast_select_fusion
  9.7 0.8 convert_bitcast_fusion
  10.8 5.5 copy.61
  16.7 47.2 %all-reduce.7.cloned.1.call-done = bf16[1024,1024]{1,0:T(8,128)(2,1)} async-done(((bf16[1024,1024]{1,0:T(8,128)(2,1)}), bf16[1024,1024]{1,0:T(8,128)(2,1)}) %all-reduce.7.cloned.1.call-update) | async-done | bytes 2097168 | tf_op jit(solution)/shard_map/psum | solution.py:12
  63.9 5.2 bitcast_subtract_fusion
  69.1 2.5 broadcast_multiply_fusion
  71.6 4.9 gather_fusion
  76.5 5.2 select_bitcast_fusion
  81.7 4.9 all-to-all-start
  87.4 92.4 %all-to-all-done = f32[1024,4,256]{0,2,1:T(8,128)} async-done(((f32[1024,4,256]{0,2,1:T(8,128)}), f32[1024,4,256]{0,2,1:T(8,128)}, u32[]{:S(2)}, u32[]{:S(2)}) %all-to-all-start) | async-done | bytes 4194336 | tf_op jit(solution)/shard_map/all_to_all | solution.py:73
  179.8 5.8 gather_fusion.1
  185.6 8.1 %gather.35 = f32[4,256,1536]{1,0,2:T(4,128)} reshape(f32[1024,6,256]{0,2,1:T(8,128)} %bitcast.115) | data formatting | bytes 12582912 | tf_op jit(solution)/shard_map/jit(_take)/gather | solution.py:30
  193.7 7.6 copy.63
  201.3 6.3 select_select_fusion.1
  207.6 8.6 %gather_fusion.2 = f32[8,256,1536]{2,1,0:T(8,128)} fusion(f32[4,256,1536]{2,1,0:T(8,128)} %select_select_fusion.1, s32[1024]{0:T(1024)S(1)} %pad_clamp_fusion.4), kind=kCustom, calls=%fused_computation.4 | custom fusion | bytes 25165856 | tf_op jit(solution)/shard_map/jit(_take)/gather | solution.py:30
  216.2 11.4 %select_select_fusion = f32[8,256,1536]{2,1,0:T(8,128)} fusion(f32[8,256,1536]{2,1,0:T(8,128)} %gather_fusion.2, pred[8]{0:T(512)(128)(4,1)S(1)} %compare_and_fusion.6, pred[8]{0:T(512)(128)(4,1)S(1)} %fusion.35), kind=kLoop, calls=%fused_computation.9 | loop fusion | flops 6291456 | bytes 25165840 | tf_op jit(solution)/shard_map/jit(_where)/select_n | solution.py:33
  227.6 5.3 all-to-all-start.1
  234.1 137.9 %all-to-all-done.1 = f32[8,256,1536]{2,1,0:T(8,128)} async-done(((f32[8,256,1536]{2,1,0:T(8,128)}), f32[8,256,1536]{2,1,0:T(8,128)}, u32[]{:S(2)}, u32[]{:S(2)}) %all-to-all-start.1) | async-done | bytes 12582944 | tf_op jit(solution)/shard_map/all_to_all | solution.py:80
  372.0 7.5 gather_fusion.5
  379.5 7.7 gather_fusion.6
  387.2 5.1 fusion
  392.3 3.2 bitcast_add_fusion
  395.5 6.0 copy.64
  401.6 6.1 copy.65
  407.7 3.0 gather_fusion.3
  410.7 2.4 copy.67
  413.1 2.5 gather.39
  415.6 1.4 select_select_fusion.5
  417.0 2.0 gather_fusion.4
  419.0 1.3 copy.88
  420.3 2.3 select_select_fusion.7
  423.3 1.4 fusion.5
  424.9 125.9 %all-reduce.11.cloned.1.call-done = f32[512,512]{0,1:T(8,128)} async-done(((f32[512,512]{0,1:T(8,128)}), f32[512,512]{0,1:T(8,128)}) %all-reduce.11.cloned.1.call-update) | async-done | bytes 1048592 | tf_op jit(solution)/shard_map/psum | solution.py:100
  550.8 1.6 copy.69
  552.3 1.4 fusion.11
  553.8 11.7 %cholesky.102 = f32[128,128]{1,0:T(8,128)S(1)} custom-call(f32[128,128]{1,0:T(8,128)S(1)} %cholesky.260), custom_call_target="Cholesky" | custom-call | tf_op jit(solution)/shard_map/jit(cholesky)/cholesky | solution.py:101
  565.6 9.8 %custom-call.30 = f32[1,128,128]{1,2,0:T(8,128)S(1)} custom-call(f32[1,128,128]{2,1,0:T(8,128)S(1)} %get-tuple-element.63), custom_call_target="InvertDiagBlocksLowerTriangular" | custom-call | tf_op jit(solution)/shard_map/jit(cholesky)/cholesky | solution.py:101
  576.0 11.7 %cholesky.213 = f32[128,128]{1,0:T(8,128)S(1)} custom-call(f32[128,128]{1,0:T(8,128)S(1)} %cholesky.264), custom_call_target="Cholesky" | custom-call | tf_op jit(solution)/shard_map/jit(cholesky)/cholesky | solution.py:101
  588.1 10.2 %custom-call.31 = f32[1,128,128]{1,2,0:T(8,128)S(1)} custom-call(f32[1,128,128]{2,1,0:T(8,128)S(1)} %get-tuple-element.61), custom_call_target="InvertDiagBlocksLowerTriangular" | custom-call | tf_op jit(solution)/shard_map/jit(cholesky)/cholesky | solution.py:101
  599.4 11.7 %cholesky.234 = f32[128,128]{1,0:T(8,128)S(1)} custom-call(f32[128,128]{1,0:T(8,128)S(1)} %cholesky.269), custom_call_target="Cholesky" | custom-call | tf_op jit(solution)/shard_map/jit(cholesky)/cholesky | solution.py:101
  611.3 9.8 %custom-call.32 = f32[1,128,128]{1,2,0:T(8,128)S(1)} custom-call(f32[1,128,128]{2,1,0:T(8,128)S(1)} %get-tuple-element.59), custom_call_target="InvertDiagBlocksLowerTriangular" | custom-call | tf_op jit(solution)/shard_map/jit(cholesky)/cholesky | solution.py:101
  621.9 11.8 %cholesky.251 = f32[128,128]{1,0:T(8,128)S(1)} custom-call(f32[128,128]{1,0:T(8,128)S(1)} %convolution_subtract_fusion.5), custom_call_target="Cholesky" | custom-call | tf_op jit(solution)/shard_map/jit(cholesky)/cholesky | solution.py:101
  633.9 0.7 compare_reduce_fusion.5
  635.1 0.7 compare_reduce_fusion.4
  639.1 8.0 %while.1 = (s32[]{:T(128)}, f32[512,512]{0,1:T(8,128)S(1)}, s32[4,2]{0,1:T(2,128)S(1)}, f32[4,128,128]{2,1,0:T(8,128)S(1)}, s32[]{:T(128)}) while((s32[]{:T(128)}, f32[512,512]{0,1:T(8,128)S(1)}, s32[4,2]{0,1:T(2,128)S(1)}, f32[4,128,128]{2,1,0:T(8,128)S(1)}, s32[]{:T(128)}) %tuple.46), condition=%wide.while_cond, body=%wide.while_body.sunk | while | flops 2 | bytes 393321 | solution.py:102
  639.7 1.3 dynamic-slice.10
  641.7 1.3 dynamic-slice.10
  643.7 1.3 dynamic-slice.10
  645.6 1.3 dynamic-slice.10
  647.0 39.3 %custom-call.33 = f32[4,128,128]{1,2,0:T(8,128)S(1)} custom-call(f32[4,128,128]{2,1,0:T(8,128)S(1)} %get-tuple-element.13), custom_call_target="InvertDiagBlocksLowerTriangular" | custom-call | tf_op jit(solution)/shard_map/triangular_solve | solution.py:102
  686.4 1.5 fusion.12
  687.9 1.5 convolution_subtract_fusion.1
  690.0 1.6 convolution_subtract_fusion.2
  692.1 1.9 convolution_subtract_fusion
  694.6 1.8 broadcast_select_fusion.1
  697.1 0.6 fusion.47
  697.7 1.3 compare_and_fusion.8
  699.1 1.3 compare_and_fusion.2
  700.5 2.6 broadcast_in_dim.369
  703.1 6.1 copy.81
  709.2 2.6 broadcast_in_dim.364
  711.8 6.2 copy.82
  718.0 46.9 %all-reduce.13.cloned.1.call-done = (f32[768,512]{0,1:T(8,128)}, f32[768,512]{0,1:T(8,128)}) async-done(((f32[768,512]{0,1:T(8,128)}, f32[768,512]{0,1:T(8,128)}), (f32[768,512]{0,1:T(8,128)}, f32[768,512]{0,1:T(8,128)})) %all-reduce.13.cloned.1.call-update) | async-done | bytes 3145744 | tf_op jit(solution)/shard_map/psum | solution.py:12
  764.9 13.1 %select_select_fusion.4 = f32[768,1536]{1,0:T(8,128)} fusion(f32[768,1536]{1,0:T(8,128)} %copy.82, f32[768,1536]{1,0:T(8,128)} %copy.81, f32[768,1536]{1,0:T(8,128)} %bitcast_add_fusion, f32[768,512]{0,1:T(8,128)} %get-tuple-element.44, f32[768,512]{0,1:T(8,128)} %get-tuple-element.45, pred[1536]{0:T(1024)(128)(4,1)S(1)} %broadcast_in_dim.367, ...), kind=kOutput, calls=%fused_computation.15 | convolution fusion | flops 7253262336 | bytes 23596032 | tf_op jit(solution)/shard_map/dot_general | solution.py:109
  (122 shorter events, 13.2 us)
Async XLA Ops:
  6.5 3.1 copy-start.2
  6.5 4.1 copy-start.1
  6.5 57.3 %all-reduce.7.cloned.1.call-start = ((), (), s32[]{:S(2)}) async-start(), calls=%async_computation.2 | async-start | bytes 4194304 | tf_op jit(solution)/shard_map/psum | solution.py:12
  10.8 53.1 %copy-start = (bf16[1,1024,1024]{2,1,0:T(8,128)(2,1)S(1)}, bf16[1,1024,1024]{2,1,0:T(8,128)(2,1)}, u32[]{:S(2)}) copy-start(bf16[1,1024,1024]{2,1,0:T(8,128)(2,1)} %param.9) | copy-start | bytes 6291460
  81.7 98.1 %all-to-all-start = ((f32[1024,4,256]{0,2,1:T(8,128)}), f32[1024,4,256]{0,2,1:T(8,128)}, u32[]{:S(2)}, u32[]{:S(2)}) async-start(f32[1024,4,256]{0,2,1:T(8,128)} %select_bitcast_fusion), calls=%async_computation | async-start | bytes 8388608 | tf_op jit(solution)/shard_map/all_to_all | solution.py:73
  227.6 144.3 %all-to-all-start.1 = ((f32[8,256,1536]{2,1,0:T(8,128)}), f32[8,256,1536]{2,1,0:T(8,128)}, u32[]{:S(2)}, u32[]{:S(2)}) async-start(f32[8,256,1536]{2,1,0:T(8,128)} %select_select_fusion), calls=%async_computation.1 | async-start | bytes 25165824 | tf_op jit(solution)/shard_map/all_to_all | solution.py:80
  233.0 317.8 %all-reduce.11.cloned.1.call-start = ((), (), s32[]{:S(2)}) async-start(), calls=%async_computation.4 | async-start | bytes 2097152 | tf_op jit(solution)/shard_map/psum | solution.py:100
  379.5 12.8 %slice-start = ((s8[4718592]{0:T(1024)(128)(4,1)}), s8[524288]{0:T(1024)(128)(4,1)S(1)}, s32[]{:S(2)}) async-start(s8[4718592]{0:T(1024)(128)(4,1)} %bitcast.121), calls=%async_computation.6 | async-start | bytes 1048576
  387.2 5.1 slice-start.1
  422.7 263.7 %all-reduce.9.cloned.1.call-start = ((), (), s32[]{:S(2)}) async-start(), calls=%async_computation.3 | async-start | bytes 3145728 | tf_op jit(solution)/shard_map/psum | solution.py:99
  424.7 340.2 %all-reduce.13.cloned.1.call-start = ((), (), s32[]{:S(2)}) async-start(), calls=%async_computation.5 | async-start | bytes 6291456 | tf_op jit(solution)/shard_map/psum | solution.py:12
Sparse Core Ops, SparseCore 0:
  9.7 54.0 all-reduce.6
  422.8 127.9 all-reduce.10
  553.2 67.9 all-reduce.8
  696.6 68.2 all-reduce.12
where the time goes:
time: 793 us; the launch traced here: 785 us
  waiting for transfers between devices  450 us (57%)
  other arithmetic  169 us (21%)
  local copies, waits for them, and re-layouts  109 us (14%)
  matrix products  28.8 us (4%)
  between operations  16.3 us (2%)
  starting transfers between devices  10.7 us (1%)
    all_to_all x1, waiting for transfers between devices, body(): lax.all_to_all(outgoing_rows, ('child', 'row'), split_axis=0, concat_axis...  138 us
    psum x1, waiting for transfers between devices, body(): diagonal_block = lax.psum(diagonal_part, ('child', 'row', 'col'))  126 us
    psum x2, waiting for transfers between devices, spread(): return lax.psum(block, axis)  94.1 us
    all_to_all x1, waiting for transfers between devices, body(): lax.all_to_all(outgoing, 'col', split_axis=1, concat_axis=1, tiled=True)  92.4 us
    another operation x15, other arithmetic, body(): factor = jnp.linalg.cholesky(diagonal_block)  79.5 us
    gather x13, local copies, waits for them, and re-layouts, select_tiles(): selected = jnp.take(source, chosen, axis=axis_pos)  61.9 us
    another operation x5, other arithmetic, body(): lax.linalg.triangular_solve(factor, panel_column, left_side=False, lower=...  39.6 us
    select_n x6, other arithmetic, select_tiles(): jnp.where(located.reshape(dims_shape), selected, jnp.zeros((), source.dty...  28 us
  transfers between devices with their start and end apart: 6, of which 5 were waited for; matrix products, arithmetic and copies ran while one was open for 21% of the time, Pallas kernels for 0%

commit v1 on v0

--- a/solution.py
+++ b/solution.py
@@ -97,7 +97,7 @@
         column.reshape(rows_dev, TILE, PANEL), row_local, row_pos, 0
     ).reshape(PANEL, PANEL)
     panel_column = lax.psum(column, "col")
-    diagonal_block = lax.psum(diagonal_part, ("child", "row", "col"))
+    diagonal_block = lax.psum(lax.psum(diagonal_part, ("row", "col")), "child")
     factor = jnp.linalg.cholesky(diagonal_block)
     panel_rows = lax.linalg.triangular_solve(
         factor, panel_column, left_side=False, lower=True, transpose_a=True

time: 793 us -> 799 us (level)
    psum x1 -> x2, waiting for transfers between devices: 126 us -> 130 us  [body(): diagonal_block = lax.psum(lax.psum(diagonal_part, ('row', 'col')), 'child')]
  transfers between devices with their start and end apart: 6 -> 7, of which waited for: 5 -> 6; matrix products, arithmetic and copies ran while one was open for 21% -> 21% of each run, Pallas kernels for 0% -> 0%
where the time goes in v1:
time: 799 us; the launch traced here: 790 us
  waiting for transfers between devices  456 us (57%)
  other arithmetic  169 us (21%)
  local copies, waits for them, and re-layouts  109 us (14%)
  matrix products  28.8 us (4%)
  between operations  16.4 us (2%)
  starting transfers between devices  10.8 us (1%)
    all_to_all x1, waiting for transfers between devices, body(): lax.all_to_all(outgoing_rows, ('child', 'row'), split_axis=0, concat_axis...  138 us
    psum x2, waiting for transfers between devices, body(): diagonal_block = lax.psum(lax.psum(diagonal_part, ('row', 'col')), 'child')  130 us
    psum x2, waiting for transfers between devices, spread(): return lax.psum(block, axis)  95.2 us
    all_to_all x1, waiting for transfers between devices, body(): lax.all_to_all(outgoing, 'col', split_axis=1, concat_axis=1, tiled=True)  92.4 us
    another operation x15, other arithmetic, body(): factor = jnp.linalg.cholesky(diagonal_block)  79.5 us
    gather x13, local copies, waits for them, and re-layouts, select_tiles(): selected = jnp.take(source, chosen, axis=axis_pos)  61.9 us
    another operation x5, other arithmetic, body(): lax.linalg.triangular_solve(factor, panel_column, left_side=False, lower=...  39.6 us
    select_n x6, other arithmetic, select_tiles(): jnp.where(located.reshape(dims_shape), selected, jnp.zeros((), source.dty...  28 us
  transfers between devices with their start and end apart: 7, of which 6 were waited for; matrix products, arithmetic and copies ran while one was open for 21% of the time, Pallas kernels for 0%

profile of v1, /device:TPU:0, one launch (start us, length us, event | category | flops | bytes accessed | tf_op | source)
XLA Modules:
  0.0 790.4 jit_solution(14623436149473355587)
XLA Ops:
  6.5 3.0 bitcast_select_fusion
  9.7 0.8 convert_bitcast_fusion
  10.8 5.5 copy.61
  16.7 47.2 %all-reduce.8.cloned.1.call-done = bf16[1024,1024]{1,0:T(8,128)(2,1)} async-done(((bf16[1024,1024]{1,0:T(8,128)(2,1)}), bf16[1024,1024]{1,0:T(8,128)(2,1)}) %all-reduce.8.cloned.1.call-update) | async-done | bytes 2097168 | tf_op jit(solution)/shard_map/psum | solution.py:12
  63.9 5.2 bitcast_subtract_fusion
  69.1 2.5 broadcast_multiply_fusion
  71.6 4.9 gather_fusion
  76.5 5.2 select_bitcast_fusion
  81.7 4.9 all-to-all-start
  87.4 92.4 %all-to-all-done = f32[1024,4,256]{0,2,1:T(8,128)} async-done(((f32[1024,4,256]{0,2,1:T(8,128)}), f32[1024,4,256]{0,2,1:T(8,128)}, u32[]{:S(2)}, u32[]{:S(2)}) %all-to-all-start) | async-done | bytes 4194336 | tf_op jit(solution)/shard_map/all_to_all | solution.py:73
  179.8 5.8 gather_fusion.1
  185.6 8.1 %gather.35 = f32[4,256,1536]{1,0,2:T(4,128)} reshape(f32[1024,6,256]{0,2,1:T(8,128)} %bitcast.115) | data formatting | bytes 12582912 | tf_op jit(solution)/shard_map/jit(_take)/gather | solution.py:30
  193.7 7.6 copy.63
  201.3 6.3 select_select_fusion.1
  207.6 8.6 %gather_fusion.2 = f32[8,256,1536]{2,1,0:T(8,128)} fusion(f32[4,256,1536]{2,1,0:T(8,128)} %select_select_fusion.1, s32[1024]{0:T(1024)S(1)} %pad_clamp_fusion.4), kind=kCustom, calls=%fused_computation.4 | custom fusion | bytes 25165856 | tf_op jit(solution)/shard_map/jit(_take)/gather | solution.py:30
  216.2 11.4 %select_select_fusion = f32[8,256,1536]{2,1,0:T(8,128)} fusion(f32[8,256,1536]{2,1,0:T(8,128)} %gather_fusion.2, pred[8]{0:T(512)(128)(4,1)S(1)} %compare_and_fusion.6, pred[8]{0:T(512)(128)(4,1)S(1)} %fusion.35), kind=kLoop, calls=%fused_computation.9 | loop fusion | flops 6291456 | bytes 25165840 | tf_op jit(solution)/shard_map/jit(_where)/select_n | solution.py:33
  227.6 5.3 all-to-all-start.1
  234.1 137.9 %all-to-all-done.1 = f32[8,256,1536]{2,1,0:T(8,128)} async-done(((f32[8,256,1536]{2,1,0:T(8,128)}), f32[8,256,1536]{2,1,0:T(8,128)}, u32[]{:S(2)}, u32[]{:S(2)}) %all-to-all-start.1) | async-done | bytes 12582944 | tf_op jit(solution)/shard_map/all_to_all | solution.py:80
  372.0 7.5 gather_fusion.5
  379.5 7.7 gather_fusion.6
  387.2 5.1 fusion
  392.3 3.2 bitcast_add_fusion
  395.5 6.0 copy.64
  401.6 6.1 copy.65
  407.7 3.0 gather_fusion.3
  410.7 2.4 copy.67
  413.1 2.5 gather.39
  415.6 1.4 select_select_fusion.5
  417.0 2.0 gather_fusion.4
  419.0 1.3 copy.88
  420.4 2.3 select_select_fusion.7
  422.8 91.0 %all-reduce.12.cloned.1.call-done = f32[512,512]{0,1:T(8,128)} async-done(((f32[512,512]{0,1:T(8,128)}), f32[512,512]{0,1:T(8,128)}) %all-reduce.12.cloned.1.call-update) | async-done | bytes 1048592 | tf_op jit(solution)/shard_map/psum | solution.py:100
  514.4 1.4 fusion.5
  516.1 39.3 %all-reduce.14.cloned.1.call-done = f32[512,512]{0,1:T(8,128)} async-done(((f32[512,512]{0,1:T(8,128)}), f32[512,512]{0,1:T(8,128)}) %all-reduce.14.cloned.1.call-update) | async-done | bytes 1048592 | tf_op jit(solution)/shard_map/psum | solution.py:100
  555.3 1.6 copy.69
  556.9 1.4 fusion.11
  558.4 11.7 %cholesky.102 = f32[128,128]{1,0:T(8,128)S(1)} custom-call(f32[128,128]{1,0:T(8,128)S(1)} %cholesky.260), custom_call_target="Cholesky" | custom-call | tf_op jit(solution)/shard_map/jit(cholesky)/cholesky | solution.py:101
  570.1 9.8 %custom-call.30 = f32[1,128,128]{1,2,0:T(8,128)S(1)} custom-call(f32[1,128,128]{2,1,0:T(8,128)S(1)} %get-tuple-element.63), custom_call_target="InvertDiagBlocksLowerTriangular" | custom-call | tf_op jit(solution)/shard_map/jit(cholesky)/cholesky | solution.py:101
  580.6 11.7 %cholesky.213 = f32[128,128]{1,0:T(8,128)S(1)} custom-call(f32[128,128]{1,0:T(8,128)S(1)} %cholesky.264), custom_call_target="Cholesky" | custom-call | tf_op jit(solution)/shard_map/jit(cholesky)/cholesky | solution.py:101
  592.7 10.2 %custom-call.31 = f32[1,128,128]{1,2,0:T(8,128)S(1)} custom-call(f32[1,128,128]{2,1,0:T(8,128)S(1)} %get-tuple-element.61), custom_call_target="InvertDiagBlocksLowerTriangular" | custom-call | tf_op jit(solution)/shard_map/jit(cholesky)/cholesky | solution.py:101
  604.0 11.7 %cholesky.234 = f32[128,128]{1,0:T(8,128)S(1)} custom-call(f32[128,128]{1,0:T(8,128)S(1)} %cholesky.269), custom_call_target="Cholesky" | custom-call | tf_op jit(solution)/shard_map/jit(cholesky)/cholesky | solution.py:101
  615.8 9.8 %custom-call.32 = f32[1,128,128]{1,2,0:T(8,128)S(1)} custom-call(f32[1,128,128]{2,1,0:T(8,128)S(1)} %get-tuple-element.59), custom_call_target="InvertDiagBlocksLowerTriangular" | custom-call | tf_op jit(solution)/shard_map/jit(cholesky)/cholesky | solution.py:101
  626.5 11.8 %cholesky.251 = f32[128,128]{1,0:T(8,128)S(1)} custom-call(f32[128,128]{1,0:T(8,128)S(1)} %convolution_subtract_fusion.5), custom_call_target="Cholesky" | custom-call | tf_op jit(solution)/shard_map/jit(cholesky)/cholesky | solution.py:101
  638.4 0.7 compare_reduce_fusion.5
  639.7 0.7 compare_reduce_fusion.4
  643.6 8.0 %while.1 = (s32[]{:T(128)}, f32[512,512]{0,1:T(8,128)S(1)}, s32[4,2]{0,1:T(2,128)S(1)}, f32[4,128,128]{2,1,0:T(8,128)S(1)}, s32[]{:T(128)}) while((s32[]{:T(128)}, f32[512,512]{0,1:T(8,128)S(1)}, s32[4,2]{0,1:T(2,128)S(1)}, f32[4,128,128]{2,1,0:T(8,128)S(1)}, s32[]{:T(128)}) %tuple.46), condition=%wide.while_cond, body=%wide.while_body.sunk | while | flops 2 | bytes 393321 | solution.py:102
  644.2 1.3 dynamic-slice.10
  646.2 1.3 dynamic-slice.10
  648.2 1.3 dynamic-slice.10
  650.2 1.3 dynamic-slice.10
  651.6 39.3 %custom-call.33 = f32[4,128,128]{1,2,0:T(8,128)S(1)} custom-call(f32[4,128,128]{2,1,0:T(8,128)S(1)} %get-tuple-element.13), custom_call_target="InvertDiagBlocksLowerTriangular" | custom-call | tf_op jit(solution)/shard_map/triangular_solve | solution.py:102
  690.9 1.5 fusion.12
  692.5 1.5 convolution_subtract_fusion.1
  694.5 1.6 convolution_subtract_fusion.2
  696.7 1.9 convolution_subtract_fusion
  699.1 1.8 broadcast_select_fusion.1
  702.3 1.3 compare_and_fusion.8
  703.6 1.3 compare_and_fusion.2
  705.0 2.6 broadcast_in_dim.369
  707.6 6.0 copy.81
  713.7 2.6 broadcast_in_dim.364
  716.4 6.2 copy.82
  722.5 48.0 %all-reduce.16.cloned.1.call-done = (f32[768,512]{0,1:T(8,128)}, f32[768,512]{0,1:T(8,128)}) async-done(((f32[768,512]{0,1:T(8,128)}, f32[768,512]{0,1:T(8,128)}), (f32[768,512]{0,1:T(8,128)}, f32[768,512]{0,1:T(8,128)})) %all-reduce.16.cloned.1.call-update) | async-done | bytes 3145744 | tf_op jit(solution)/shard_map/psum | solution.py:12
  770.5 13.1 %select_select_fusion.4 = f32[768,1536]{1,0:T(8,128)} fusion(f32[768,1536]{1,0:T(8,128)} %copy.82, f32[768,1536]{1,0:T(8,128)} %copy.81, f32[768,1536]{1,0:T(8,128)} %bitcast_add_fusion, f32[768,512]{0,1:T(8,128)} %get-tuple-element.44, f32[768,512]{0,1:T(8,128)} %get-tuple-element.45, pred[1536]{0:T(1024)(128)(4,1)S(1)} %broadcast_in_dim.367, ...), kind=kOutput, calls=%fused_computation.15 | convolution fusion | flops 7253262336 | bytes 23596032 | tf_op jit(solution)/shard_map/dot_general | solution.py:109
  (125 shorter events, 13.9 us)
Async XLA Ops:
  6.5 3.1 copy-start.2
  6.5 4.1 copy-start.1
  6.5 57.3 %all-reduce.8.cloned.1.call-start = ((), (), s32[]{:S(2)}) async-start(), calls=%async_computation.2 | async-start | bytes 4194304 | tf_op jit(solution)/shard_map/psum | solution.py:12
  10.8 53.1 %copy-start = (bf16[1,1024,1024]{2,1,0:T(8,128)(2,1)S(1)}, bf16[1,1024,1024]{2,1,0:T(8,128)(2,1)}, u32[]{:S(2)}) copy-start(bf16[1,1024,1024]{2,1,0:T(8,128)(2,1)} %param.9) | copy-start | bytes 6291460
  81.7 98.1 %all-to-all-start = ((f32[1024,4,256]{0,2,1:T(8,128)}), f32[1024,4,256]{0,2,1:T(8,128)}, u32[]{:S(2)}, u32[]{:S(2)}) async-start(f32[1024,4,256]{0,2,1:T(8,128)} %select_bitcast_fusion), calls=%async_computation | async-start | bytes 8388608 | tf_op jit(solution)/shard_map/all_to_all | solution.py:73
  227.6 144.3 %all-to-all-start.1 = ((f32[8,256,1536]{2,1,0:T(8,128)}), f32[8,256,1536]{2,1,0:T(8,128)}, u32[]{:S(2)}, u32[]{:S(2)}) async-start(f32[8,256,1536]{2,1,0:T(8,128)} %select_select_fusion), calls=%async_computation.1 | async-start | bytes 25165824 | tf_op jit(solution)/shard_map/all_to_all | solution.py:80
  233.0 280.9 %all-reduce.12.cloned.1.call-start = ((), (), s32[]{:S(2)}) async-start(), calls=%async_computation.4 | async-start | bytes 2097152 | tf_op jit(solution)/shard_map/psum | solution.py:100
  379.5 12.8 %slice-start = ((s8[4718592]{0:T(1024)(128)(4,1)}), s8[524288]{0:T(1024)(128)(4,1)S(1)}, s32[]{:S(2)}) async-start(s8[4718592]{0:T(1024)(128)(4,1)} %bitcast.121), calls=%async_computation.7 | async-start | bytes 1048576
  387.2 5.1 slice-start.1
  422.7 132.6 %all-reduce.14.cloned.1.call-start = ((), (), s32[]{:S(2)}) async-start(), calls=%async_computation.5 | async-start | bytes 2097152 | tf_op jit(solution)/shard_map/psum | solution.py:100
  513.9 177.1 %all-reduce.10.cloned.1.call-start = ((), (), s32[]{:S(2)}) async-start(), calls=%async_computation.3 | async-start | bytes 3145728 | tf_op jit(solution)/shard_map/psum | solution.py:99
  515.8 254.7 %all-reduce.16.cloned.1.call-start = ((), (), s32[]{:S(2)}) async-start(), calls=%async_computation.6 | async-start | bytes 6291456 | tf_op jit(solution)/shard_map/psum | solution.py:12
Sparse Core Ops, SparseCore 0:
  9.7 54.0 all-reduce.7
  422.9 90.9 all-reduce.11
  516.1 39.1 all-reduce.13
  557.6 69.1 all-reduce.9
  701.1 69.3 all-reduce.15
